TPU v7x, 32 devices: a whole 2x2x4 slice. The times are simulated.
32 devices in a mesh: prow: 4 (over y, x), pcol: 8 (over z, core).
Axes of the slice: x: 2, y: 2, z: 4, core: 2. Of those that a mesh axis runs over, the one named last changes fastest.
Arguments:
- anc_inverse: bfloat16 [6, 1024, 3, 2048], P(None, 'prow', None, 'pcol'), may hold values from -0.078125 to 0.078125
- panel: bfloat16 [3, 6, 4, 256, 512], P(None, None, 'prow', 'pcol'), may hold values from -1.1953125 to 1.1953125
- tile_mask: int32 [3, 24], replicated, may hold values 0 or 1
- diag_inverse: float32 [3, 512, 512], P(None, ('prow', 'pcol')), may hold values from -6 to 6
Outputs:
- block_column: bfloat16 [3, 6, 4, 256, 512], P(None, None, 'prow', 'pcol')
- diag_block: float32 [3, 512, 512], P(None, ('prow', 'pcol'))
All inputs are finite; a program needn't handle non-finite values.
Results may differ from a plain program's by a relative error of at most 0.0017.
Values may be sent and summed in bfloat16 or wider, within the bound.
No kernel may reach another device: no remote copies, remote signals or barrier semaphores. Data moves between devices by JAX's collectives and lax.ppermute only.
A program may use at most 128 MiB of HBM per device.

v0:
```python
import functools

import jax
import jax.numpy as jnp
from jax import lax
from jax.experimental import pallas as pl
from jax.experimental.pallas import tpu as pltpu
from jax.sharding import PartitionSpec as P


CORES = 2


def by_col(x, n_col, k):
    return lax.ppermute(x, "pcol", [(q, q ^ k) for q in range(n_col)])


def by_row(x, n_row, k):
    return lax.ppermute(x, "prow", [(p, p ^ k) for p in range(n_row)])


def pick(x, index, axis):
    return lax.dynamic_index_in_dim(x, index, axis=axis, keepdims=False)


def product_kernel(n_row, count, pos, *refs):
    blocks = [refs[i * n_row : (i + 1) * n_row] for i in range(count)]
    pieces, refs = refs[count * n_row : (count + 1) * n_row], refs[(count + 1) * n_row :]
    outs, held = refs[:count], refs[count]
    place, turn = pos[0], pos[1]
    n_line, tile_cols, rows, _ = pieces[0].shape
    tile_rows = blocks[0][0].shape[0]
    tile = n_line * rows
    for k in range(n_row):
        for j in range(n_line):
            start = pl.multiple_of((place ^ j) * rows, rows)
            for b in range(tile_cols):
                base = pl.multiple_of(((k ^ turn) * tile_cols + b) * tile, tile)
                held[pl.ds(base + start, rows), :] = pieces[k][j, b]
    for out, wide in zip(outs, blocks):
        wide = jnp.concatenate(
            [
                block[:, b].reshape(tile_rows * rows, tile)
                for block in wide
                for b in range(tile_cols)
            ],
            axis=1,
        )
        out[...] = jnp.dot(wide, held[...], preferred_element_type=jnp.float32)


def product(pos, blocks, pieces):
    count, n_row = len(blocks), len(pieces)
    tile_rows, tile_cols, rows, tile = blocks[0][0].shape
    half = pieces[0].shape[-1]
    height, depth = tile_rows * rows, n_row * tile_cols * tile
    vmem = pl.BlockSpec(memory_space=pltpu.VMEM)
    return pl.pallas_call(
        functools.partial(product_kernel, n_row, count),
        out_shape=[jax.ShapeDtypeStruct((height, half), jnp.float32)] * count,
        in_specs=[pl.BlockSpec(memory_space=pltpu.SMEM)] + [vmem] * ((count + 1) * n_row),
        out_specs=[vmem] * count,
        scratch_shapes=[pltpu.VMEM((depth, half), jnp.bfloat16)],
        cost_estimate=pl.CostEstimate(
            flops=2 * count * height * depth * half,
            bytes_accessed=2 * depth * (count * height + half) + 4 * count * height * half,
            transcendentals=0,
        ),
    )(pos, *[x for block in blocks for x in block], *pieces)


def share_panel(x, group, groups, members, n_col):
    got = [pick(x, group, 1)]
    for k in range(1, groups):
        got.append(by_col(pick(x, group ^ k, 1), n_col, k * members * CORES))
    got = jnp.stack(got)
    all_got = [got] + [by_col(got, n_col, m * CORES) for m in range(1, members)]
    return jnp.stack(all_got, axis=1).reshape((-1,) + got.shape[1:])


def share_rows(piece, n_row):
    return [piece] + [by_row(piece, n_row, k) for k in range(1, n_row)]


def reduce_groups(parts, groups, members, n_col):
    k = 1
    while k < groups:
        parts = [
            parts[r] + by_col(parts[r + 1], n_col, k * members * CORES)
            for r in range(0, len(parts), 2)
        ]
        k *= 2
    return parts[0]


def spread_sum(x, place, count, move):
    total = pick(x, place, 1)
    for k in range(1, count):
        total = total + move(pick(x, place ^ k, 1), k)
    return total


def reduce_rows(value, row_pos, n_row):
    x = value.reshape(1, n_row, -1, value.shape[-1])
    return spread_sum(x, row_pos, n_row, lambda y, k: by_row(y, n_row, k))


def reduce_places(values, place, n_line, n_col):
    x = jnp.concatenate(values)
    x = x.reshape(x.shape[0], n_line, -1, x.shape[-1])
    return spread_sum(x, place, n_line, lambda y, k: by_col(y, n_col, k * CORES))


def step(anc_inverse, panel, tile_mask, diag_inverse):
    n_row = lax.axis_size("prow")
    n_col = lax.axis_size("pcol")
    row_pos = lax.axis_index("prow")
    col_pos = lax.axis_index("pcol")
    place, core = col_pos // CORES, col_pos % CORES
    sets, tile_rows, _, sub, width = panel.shape
    tiles = tile_mask.shape[1]
    n_line = n_col // CORES
    members = n_row // CORES
    groups = n_line // members
    group, within = place // members, place % members
    half = width // CORES
    row_ids = jnp.arange(tile_rows, dtype=jnp.int32) * n_row + row_pos
    hits = (row_ids[:, None] == jnp.arange(tiles, dtype=jnp.int32)[None, :]).astype(jnp.int32)
    row_mask = jnp.sum(tile_mask[:, None, :] * hits[None], axis=2)
    keep = row_mask.astype(jnp.bfloat16)[:, :, None, None]
    keep32 = keep.astype(jnp.float32)
    masked = panel[:, :, 0] * keep
    tile_cols = tile_rows // groups
    anc = jnp.transpose(anc_inverse, (0, 2, 1, 3))
    anc = anc.reshape(tile_rows, tile_cols, groups, members, CORES * sub, -1)
    def chosen(m, r):
        x = lax.dynamic_index_in_dim(anc, group ^ r, axis=2, keepdims=False)
        return lax.dynamic_index_in_dim(x, within ^ m, axis=2, keepdims=False)

    blocks = []
    for r in range(groups):
        kept = [chosen(m, r) for m in range(members)]
        kept = kept[:1] + [by_col(kept[m], n_col, m * CORES) for m in range(1, members)]
        wide = []
        for x in kept:
            wide += [x, by_col(x, n_col, 1)]
        blocks.append(wide)
    other = by_col(masked, n_col, 1)
    both = jnp.concatenate(
        [jnp.where(core == 0, masked, other), jnp.where(core == 0, other, masked)], axis=2
    )
    narrow = lax.dynamic_slice_in_dim(both, core * half, half, axis=3)
    narrow = narrow.reshape(sets, tile_cols, groups, CORES * sub, half)
    pos = jnp.stack([place, row_pos ^ (col_pos % n_row)]).astype(jnp.int32)
    outs, values, diags = [], [], []
    for s in range(sets):
        piece = share_panel(narrow[s], group, groups, members, n_col)
        pieces = share_rows(piece, n_row)
        if s:
            parts = product(pos, blocks, pieces)
        else:
            parts = product(pos, blocks[-1:], pieces)
            parts = product(pos, blocks[:-1], pieces) + parts
        total = reduce_groups(parts, groups, members, n_col)
        total = total.reshape(tile_rows, CORES, sub, half)
        image = (-total * keep32[s, :, None]).astype(jnp.bfloat16)
        stay, leave = pick(image, core, 1), pick(image, 1 - core, 1)
        came = by_col(leave, n_col, 1)
        outs.append(
            jnp.concatenate(
                [jnp.where(core == 0, stay, came), jnp.where(core == 0, came, stay)], axis=-1
            )
        )
        value = jnp.einsum(
            "axw,axv->wv", both[s], image.reshape(tile_rows, -1, half),
            preferred_element_type=jnp.float32,
        )
        values.append(reduce_rows(value, row_pos, n_row))
        if s in (sets - 2, sets - 1):
            diags.append(reduce_places(values, place, n_line, n_col))
            values = []
    x = jnp.concatenate(diags)
    x = x.reshape(sets, CORES, -1, half)
    stay, leave = pick(x, core, 1), pick(x, 1 - core, 1)
    came = by_col(leave, n_col, 1)
    diag = jnp.concatenate(
        [jnp.where(core == 0, stay, came), jnp.where(core == 0, came, stay)], axis=-1
    )
    block_column = jnp.stack(outs)[:, :, None]
    return (block_column, diag_inverse - diag)


def solution(mesh):
    in_specs = (
        P(None, "prow", None, "pcol"),
        P(None, None, "prow", "pcol", None),
        P(),
        P(None, ("prow", "pcol"), None),
    )
    out_specs = (P(None, None, "prow", "pcol", None), P(None, ("prow", "pcol"), None))
    return jax.shard_map(step, mesh=mesh, in_specs=in_specs, out_specs=out_specs, check_vma=False)
```

profile of v0, /device:TPU:0, one launch (start us, length us, event | category | flops | bytes accessed | tf_op | source)
XLA Modules:
  0.0 174.1 jit_solution(13820618255394316209)
XLA Ops:
  4.0 2.9 %dynamic-slice_bitcast_fusion = (bf16[6,3,64,256]{3,2,1,0:T(8,128)(2,1)}, bf16[6,3,64,256]{3,2,1,0:T(8,128)(2,1)S(1)}, bf16[6,3,64,256]{3,2,1,0:T(8,128)(2,1)}, bf16[6,3,64,256]{3,2,1,0:T(8,128)(2,1)S(1)}) fusion(bf16[6,3,2,2,64,256]{5,4,3,2,1,0:T(8,128)(2,1)} %bitcast.175, s32[]{:T(128)S(6)} %select_n.180, s32[]{:T(128)S(6)} %select_n.174, ...), kind=kLoop, calls=%fused_computation.12 | loop fusion | bytes 4718608 | tf_op jit(solution)/shard_map/jit(dynamic_index_in_dim)/squeeze | solution.py:138
  6.9 2.6 %collective-permute-start.10 = (bf16[6,3,64,256]{3,2,1,0:T(8,128)(2,1)}, bf16[6,3,64,256]{3,2,1,0:T(8,128)(2,1)S(1)}, u32[]{:S(2)}, u32[]{:S(2)}) collective-permute-start(bf16[6,3,64,256]{3,2,1,0:T(8,128)(2,1)} %get-tuple-element.18), channel_id=1, source_target_pairs={{0,2},{1,3},{2,0},{3,1},{4,6},{5,7},{6,4},{7,5},{8,10},{9,11},{10,... | collective-permute-start | bytes 1769480 | tf_op jit(solution)/shard_map/ppermute | solution.py:15
  12.5 2.8 %collective-permute-start.4 = (bf16[3,64,256]{2,1,0:T(8,128)(2,1)S(1)}, bf16[3,64,256]{2,1,0:T(8,128)(2,1)S(1)}, u32[]{:S(2)}, u32[]{:S(2)}) collective-permute-start(bf16[3,64,256]{2,1,0:T(8,128)(2,1)S(1)} %get-tuple-element.51), channel_id=1, source_target_pairs={{0,4},{1,5},{2,6},{3,7},{4,0},{5,1},{6,2},{7,3},{8,12},{9,13},{10,... | collective-permute-start | bytes 294920 | tf_op jit(solution)/shard_map/ppermute | solution.py:15
  15.3 10.6 %collective-permute-done.10.refs_2_.refs_6_ = bf16[6,3,64,256]{3,2,1,0:T(8,128)(2,1)S(1)} collective-permute-done((bf16[6,3,64,256]{3,2,1,0:T(8,128)(2,1)}, bf16[6,3,64,256]{3,2,1,0:T(8,128)(2,1)S(1)}, u32[]{:S(2)}, u32[]{:S(2)}) %collective-permute-start.10) | collective-permute-done | bytes 589856 | tf_op jit(solution)/shard_map/ppermute | solution.py:15
  28.2 12.3 %collective-permute-done.1.refs_2_ = bf16[6,3,64,256]{3,2,1,0:T(8,128)(2,1)S(1)} collective-permute-done((bf16[6,3,64,256]{3,2,1,0:T(8,128)(2,1)}, bf16[6,3,64,256]{3,2,1,0:T(8,128)(2,1)S(1)}, u32[]{:S(2)}, u32[]{:S(2)}) %collective-permute-start.1) | collective-permute-done | bytes 589856 | tf_op jit(solution)/shard_map/ppermute | solution.py:15
  45.5 3.5 %collective-permute-done.21 = bf16[3,64,256]{2,1,0:T(8,128)(2,1)S(1)} collective-permute-done((bf16[3,64,256]{2,1,0:T(8,128)(2,1)S(1)}, bf16[3,64,256]{2,1,0:T(8,128)(2,1)S(1)}, u32[]{:S(2)}, u32[]{:S(2)}) %collective-permute-start.21) | collective-permute-done | bytes 98336 | tf_op jit(solution)/shard_map/ppermute | solution.py:15
  49.2 2.9 %collective-permute-done.5 = bf16[2,3,64,256]{3,2,1,0:T(8,128)(2,1)S(1)} collective-permute-done((bf16[2,3,64,256]{3,2,1,0:T(8,128)(2,1)S(1)}, bf16[2,3,64,256]{3,2,1,0:T(8,128)(2,1)S(1)}, u32[]{:S(2)}, u32[]{:S(2)}) %collective-permute-start.5) | collective-permute-done | bytes 196640 | tf_op jit(solution)/shard_map/ppermute | solution.py:15
  52.6 4.2 %collective-permute-done.15 = bf16[2,3,64,256]{3,2,1,0:T(8,128)(2,1)S(1)} collective-permute-done((bf16[2,3,64,256]{3,2,1,0:T(8,128)(2,1)S(1)}, bf16[2,3,64,256]{3,2,1,0:T(8,128)(2,1)S(1)}, u32[]{:S(2)}, u32[]{:S(2)}) %collective-permute-start.15) | collective-permute-done | bytes 196640 | tf_op jit(solution)/shard_map/ppermute | solution.py:15
  65.6 2.7 %collective-permute-done.6.refs_5_ = bf16[4,3,64,256]{3,2,1,0:T(8,128)(2,1)} collective-permute-done((bf16[4,3,64,256]{3,2,1,0:T(8,128)(2,1)S(1)}, bf16[4,3,64,256]{3,2,1,0:T(8,128)(2,1)}, u32[]{:S(2)}, u32[]{:S(2)}) %collective-permute-start.6) | collective-permute-done | bytes 393248 | tf_op jit(solution)/shard_map/ppermute | solution.py:19
  68.3 3.2 %collective-permute-start.18 = (bf16[4,3,64,256]{3,2,1,0:T(8,128)(2,1)}, bf16[4,3,64,256]{3,2,1,0:T(8,128)(2,1)}, u32[]{:S(2)}, u32[]{:S(2)}) collective-permute-start(bf16[4,3,64,256]{3,2,1,0:T(8,128)(2,1)} %bitcast.30.refs_8_), channel_id=1, source_target_pairs={{0,24},{8,16},{16,8},{24,0},{1,25},{9,17},{17,9},{25,1},{2,26},{10... | collective-permute-start | bytes 1179656 | tf_op jit(solution)/shard_map/ppermute | solution.py:19
  72.5 7.1 %collective-permute-done.7.refs_6_ = bf16[4,3,64,256]{3,2,1,0:T(8,128)(2,1)S(1)} collective-permute-done((bf16[4,3,64,256]{3,2,1,0:T(8,128)(2,1)S(1)}, bf16[4,3,64,256]{3,2,1,0:T(8,128)(2,1)S(1)}, u32[]{:S(2)}, u32[]{:S(2)}) %collective-permute-start.7) | collective-permute-done | bytes 393248 | tf_op jit(solution)/shard_map/ppermute | solution.py:19
  81.5 3.7 %collective-permute-done.16.refs_9_ = bf16[4,3,64,256]{3,2,1,0:T(8,128)(2,1)} collective-permute-done((bf16[4,3,64,256]{3,2,1,0:T(8,128)(2,1)}, bf16[4,3,64,256]{3,2,1,0:T(8,128)(2,1)}, u32[]{:S(2)}, u32[]{:S(2)}) %collective-permute-start.16) | collective-permute-done | bytes 393248 | tf_op jit(solution)/shard_map/ppermute | solution.py:19
  85.2 3.2 %collective-permute-start.25 = (bf16[4,3,64,256]{3,2,1,0:T(8,128)(2,1)S(1)}, bf16[4,3,64,256]{3,2,1,0:T(8,128)(2,1)}, u32[]{:S(2)}, u32[]{:S(2)}) collective-permute-start(bf16[4,3,64,256]{3,2,1,0:T(8,128)(2,1)S(1)} %bitcast.178), channel_id=1, source_target_pairs={{0,24},{8,16},{16,8},{24,0},{1,25},{9,17},{17,9},{25,1},{2,26},{10... | collective-permute-start | bytes 1179656 | tf_op jit(solution)/shard_map/ppermute | solution.py:19
  89.0 3.8 %shard_map.60 = f32[384,256]{1,0:T(8,128)} custom-call(s32[2]{0:T(128)} %pad_add_fusion.pos, bf16[6,3,64,256]{3,2,1,0:T(8,128)(2,1)} %copy-done.1, bf16[6,3,64,256]{3,2,1,0:T(8,128)(2,1)} %copy-done.5, bf16[6,3,64,256]{3,2,1,0:T(8,128)(2,1)} %copy-done.4, bf16[6,3,64,256]{3,2,1,0:T(8,128)(2,1)} %copy-done.7, bf16[4,3,64,256]{3,2,1,0:T(8,128)(2,1)} %bitcast.173, ...), custom_call_target="tpu_custom_call" | custom-call | flops 603979776 | bytes 4325376 | tf_op jit(solution)/shard_map/pallas_call | solution.py:58
  92.8 3.6 %collective-permute-done.17.refs_10_ = bf16[4,3,64,256]{3,2,1,0:T(8,128)(2,1)S(1)} collective-permute-done((bf16[4,3,64,256]{3,2,1,0:T(8,128)(2,1)}, bf16[4,3,64,256]{3,2,1,0:T(8,128)(2,1)S(1)}, u32[]{:S(2)}, u32[]{:S(2)}) %collective-permute-start.17) | collective-permute-done | bytes 393248 | tf_op jit(solution)/shard_map/ppermute | solution.py:19
  98.9 5.2 %shard_map.61 = (f32[384,256]{1,0:T(8,128)}, f32[384,256]{1,0:T(8,128)}) custom-call(s32[2]{0:T(128)} %pad_add_fusion.pos, bf16[6,3,64,256]{3,2,1,0:T(8,128)(2,1)} %copy-done, bf16[6,3,64,256]{3,2,1,0:T(8,128)(2,1)} %copy-done.3, bf16[6,3,64,256]{3,2,1,0:T(8,128)(2,1)} %copy-done.2, bf16[6,3,64,256]{3,2,1,0:T(8,128)(2,1)} %copy-done.6, ...), custom_call_target="tpu_custom_call" | custom-call | flops 1207959552 | bytes 7077888 | tf_op jit(solution)/shard_map/pallas_call | solution.py:58
  105.6 4.0 %collective-permute-done.24.refs_10_ = bf16[4,3,64,256]{3,2,1,0:T(8,128)(2,1)} collective-permute-done((bf16[4,3,64,256]{3,2,1,0:T(8,128)(2,1)S(1)}, bf16[4,3,64,256]{3,2,1,0:T(8,128)(2,1)}, u32[]{:S(2)}, u32[]{:S(2)}) %collective-permute-start.24) | collective-permute-done | bytes 393248 | tf_op jit(solution)/shard_map/ppermute | solution.py:19
  109.7 5.2 %shard_map.62 = (f32[384,256]{1,0:T(8,128)}, f32[384,256]{1,0:T(8,128)}) custom-call(s32[2]{0:T(128)} %pad_add_fusion.pos, bf16[6,3,64,256]{3,2,1,0:T(8,128)(2,1)} %copy-done, bf16[6,3,64,256]{3,2,1,0:T(8,128)(2,1)} %copy-done.3, bf16[6,3,64,256]{3,2,1,0:T(8,128)(2,1)} %copy-done.2, bf16[6,3,64,256]{3,2,1,0:T(8,128)(2,1)} %copy-done.6, ...), custom_call_target="tpu_custom_call" | custom-call | flops 1207959552 | bytes 7077888 | tf_op jit(solution)/shard_map/pallas_call | solution.py:58
  114.8 2.5 %collective-permute-start.26 = (f32[384,256]{1,0:T(8,128)}, f32[384,256]{1,0:T(8,128)S(1)}, u32[]{:S(2)}, u32[]{:S(2)}) collective-permute-start(f32[384,256]{1,0:T(8,128)} %get-tuple-element.9), channel_id=1, source_target_pairs={{0,4},{1,5},{2,6},{3,7},{4,0},{5,1},{6,2},{7,3},{8,12},{9,13},{10,... | collective-permute-start | bytes 1179656 | tf_op jit(solution)/shard_map/ppermute | solution.py:15
  117.4 3.7 %shard_map.59 = f32[384,256]{1,0:T(8,128)} custom-call(s32[2]{0:T(128)} %pad_add_fusion.pos, bf16[6,3,64,256]{3,2,1,0:T(8,128)(2,1)} %copy-done, bf16[6,3,64,256]{3,2,1,0:T(8,128)(2,1)} %copy-done.3, bf16[6,3,64,256]{3,2,1,0:T(8,128)(2,1)} %copy-done.2, bf16[6,3,64,256]{3,2,1,0:T(8,128)(2,1)} %copy-done.6, bf16[4,3,64,256]{3,2,1,0:T(8,128)(2,1)} %bitcast.174, ...), custom_call_target="tpu_custom_call" | custom-call | flops 603979776 | bytes 4325376 | tf_op jit(solution)/shard_map/pallas_call | solution.py:58
  121.1 7.9 %collective-permute-done.12 = f32[384,256]{1,0:T(8,128)S(1)} collective-permute-done((f32[384,256]{1,0:T(8,128)}, f32[384,256]{1,0:T(8,128)S(1)}, u32[]{:S(2)}, u32[]{:S(2)}) %collective-permute-start.12) | collective-permute-done | bytes 393248 | tf_op jit(solution)/shard_map/ppermute | solution.py:15
  132.6 4.8 %collective-permute-done.19 = f32[384,256]{1,0:T(8,128)S(1)} collective-permute-done((f32[384,256]{1,0:T(8,128)}, f32[384,256]{1,0:T(8,128)S(1)}, u32[]{:S(2)}, u32[]{:S(2)}) %collective-permute-start.19) | collective-permute-done | bytes 393248 | tf_op jit(solution)/shard_map/ppermute | solution.py:15
  138.0 3.7 %collective-permute-done.26 = f32[384,256]{1,0:T(8,128)S(1)} collective-permute-done((f32[384,256]{1,0:T(8,128)}, f32[384,256]{1,0:T(8,128)S(1)}, u32[]{:S(2)}, u32[]{:S(2)}) %collective-permute-start.26) | collective-permute-done | bytes 393248 | tf_op jit(solution)/shard_map/ppermute | solution.py:15
  158.0 3.3 %collective-permute-start.41 = (f32[1,32,256]{2,1,0:T(8,128)S(1)}, f32[1,32,256]{2,1,0:T(8,128)S(1)}, u32[]{:S(2)}, u32[]{:S(2)}) collective-permute-start(f32[1,32,256]{2,1,0:T(8,128)S(1)} %get-tuple-element.64), channel_id=1, source_target_pairs={{0,4},{1,5},{2,6},{3,7},{4,0},{5,1},{6,2},{7,3},{8,12},{9,13},{10,... | collective-permute-start | bytes 98312 | tf_op jit(solution)/shard_map/ppermute | solution.py:15
  (168 shorter events, 63.5 us)
Async XLA Ops:
  6.9 19.1 %collective-permute-start.10 = (bf16[6,3,64,256]{3,2,1,0:T(8,128)(2,1)}, bf16[6,3,64,256]{3,2,1,0:T(8,128)(2,1)S(1)}, u32[]{:S(2)}, u32[]{:S(2)}) collective-permute-start(bf16[6,3,64,256]{3,2,1,0:T(8,128)(2,1)} %get-tuple-element.18), channel_id=1, source_target_pairs={{0,2},{1,3},{2,0},{3,1},{4,6},{5,7},{6,4},{7,5},{8,10},{9,11},{10,... | collective-permute-start | bytes 1769480 | tf_op jit(solution)/shard_map/ppermute | solution.py:15
  9.5 31.6 %collective-permute-start.9 = (bf16[6,3,64,256]{3,2,1,0:T(8,128)(2,1)S(1)}, bf16[6,3,64,256]{3,2,1,0:T(8,128)(2,1)S(1)}, u32[]{:S(2)}, u32[]{:S(2)}) collective-permute-start(bf16[6,3,64,256]{3,2,1,0:T(8,128)(2,1)S(1)} %get-tuple-element.19.refs_0_.refs_4_), channel_id=1, source_target_pairs={{0,1},{1,0},{2,3},{3,2},{4,5},{5,4},{6,7},{7,6},{8,9},{9,8},{10,11... | collective-permute-start | bytes 1769480 | tf_op jit(solution)/shard_map/ppermute | solution.py:15
  9.7 30.8 %collective-permute-start.1 = (bf16[6,3,64,256]{3,2,1,0:T(8,128)(2,1)}, bf16[6,3,64,256]{3,2,1,0:T(8,128)(2,1)S(1)}, u32[]{:S(2)}, u32[]{:S(2)}) collective-permute-start(bf16[6,3,64,256]{3,2,1,0:T(8,128)(2,1)} %get-tuple-element.20), channel_id=1, source_target_pairs={{0,2},{1,3},{2,0},{3,1},{4,6},{5,7},{6,4},{7,5},{8,10},{9,11},{10,... | collective-permute-start | bytes 1769480 | tf_op jit(solution)/shard_map/ppermute | solution.py:15
  10.0 49.2 %collective-permute-start = (bf16[6,3,64,256]{3,2,1,0:T(8,128)(2,1)S(1)}, bf16[6,3,64,256]{3,2,1,0:T(8,128)(2,1)S(1)}, u32[]{:S(2)}, u32[]{:S(2)}) collective-permute-start(bf16[6,3,64,256]{3,2,1,0:T(8,128)(2,1)S(1)} %get-tuple-element.21.refs_0_), channel_id=1, source_target_pairs={{0,1},{1,0},{2,3},{3,2},{4,5},{5,4},{6,7},{7,6},{8,9},{9,8},{10,11... | collective-permute-start | bytes 1769480 | tf_op jit(solution)/shard_map/ppermute | solution.py:15
  12.5 28.0 %collective-permute-start.4 = (bf16[3,64,256]{2,1,0:T(8,128)(2,1)S(1)}, bf16[3,64,256]{2,1,0:T(8,128)(2,1)S(1)}, u32[]{:S(2)}, u32[]{:S(2)}) collective-permute-start(bf16[3,64,256]{2,1,0:T(8,128)(2,1)S(1)} %get-tuple-element.51), channel_id=1, source_target_pairs={{0,4},{1,5},{2,6},{3,7},{4,0},{5,1},{6,2},{7,3},{8,12},{9,13},{10,... | collective-permute-start | bytes 294920 | tf_op jit(solution)/shard_map/ppermute | solution.py:15
  26.0 17.2 %collective-permute-start.14 = (bf16[3,64,256]{2,1,0:T(8,128)(2,1)S(1)}, bf16[3,64,256]{2,1,0:T(8,128)(2,1)S(1)}, u32[]{:S(2)}, u32[]{:S(2)}) collective-permute-start(bf16[3,64,256]{2,1,0:T(8,128)(2,1)S(1)} %get-tuple-element.55), channel_id=1, source_target_pairs={{0,4},{1,5},{2,6},{3,7},{4,0},{5,1},{6,2},{7,3},{8,12},{9,13},{10,... | collective-permute-start | bytes 294920 | tf_op jit(solution)/shard_map/ppermute | solution.py:15
  40.5 21.8 %collective-permute-start.11 = (bf16[6,3,64,256]{3,2,1,0:T(8,128)(2,1)S(1)}, bf16[6,3,64,256]{3,2,1,0:T(8,128)(2,1)S(1)}, u32[]{:S(2)}, u32[]{:S(2)}) collective-permute-start(bf16[6,3,64,256]{3,2,1,0:T(8,128)(2,1)S(1)} %collective-permute-done.10.refs_2_.refs_6_), channel_id=1, source_target_pairs={{0,1},{1,0},{2,3},{3,2},{4,5},{5,4},{6,7},{7,6},{8,9},{9,8},{10,11... | collective-permute-start | bytes 1769480 | tf_op jit(solution)/shard_map/ppermute | solution.py:15
  40.5 22.4 %collective-permute-start.2 = (bf16[6,3,64,256]{3,2,1,0:T(8,128)(2,1)S(1)}, bf16[6,3,64,256]{3,2,1,0:T(8,128)(2,1)S(1)}, u32[]{:S(2)}, u32[]{:S(2)}) collective-permute-start(bf16[6,3,64,256]{3,2,1,0:T(8,128)(2,1)S(1)} %collective-permute-done.1.refs_2_), channel_id=1, source_target_pairs={{0,1},{1,0},{2,3},{3,2},{4,5},{5,4},{6,7},{7,6},{8,9},{9,8},{10,11... | collective-permute-start | bytes 1769480 | tf_op jit(solution)/shard_map/ppermute | solution.py:15
  56.8 11.5 %collective-permute-start.6 = (bf16[4,3,64,256]{3,2,1,0:T(8,128)(2,1)S(1)}, bf16[4,3,64,256]{3,2,1,0:T(8,128)(2,1)}, u32[]{:S(2)}, u32[]{:S(2)}) collective-permute-start(bf16[4,3,64,256]{3,2,1,0:T(8,128)(2,1)S(1)} %bitcast.170), channel_id=1, source_target_pairs={{0,8},{8,0},{16,24},{24,16},{1,9},{9,1},{17,25},{25,17},{2,10},{10... | collective-permute-start | bytes 1179656 | tf_op jit(solution)/shard_map/ppermute | solution.py:19
  59.3 20.3 %collective-permute-start.7 = (bf16[4,3,64,256]{3,2,1,0:T(8,128)(2,1)S(1)}, bf16[4,3,64,256]{3,2,1,0:T(8,128)(2,1)S(1)}, u32[]{:S(2)}, u32[]{:S(2)}) collective-permute-start(bf16[4,3,64,256]{3,2,1,0:T(8,128)(2,1)S(1)} %bitcast.171), channel_id=1, source_target_pairs={{0,16},{8,24},{16,0},{24,8},{1,17},{9,25},{17,1},{25,9},{2,18},{10... | collective-permute-start | bytes 1179656 | tf_op jit(solution)/shard_map/ppermute | solution.py:19
  60.8 18.7 %collective-permute-start.8 = (bf16[4,3,64,256]{3,2,1,0:T(8,128)(2,1)S(1)}, bf16[4,3,64,256]{3,2,1,0:T(8,128)(2,1)S(1)}, u32[]{:S(2)}, u32[]{:S(2)}) collective-permute-start(bf16[4,3,64,256]{3,2,1,0:T(8,128)(2,1)S(1)} %bitcast.172), channel_id=1, source_target_pairs={{0,24},{8,16},{16,8},{24,0},{1,25},{9,17},{17,9},{25,1},{2,26},{10... | collective-permute-start | bytes 1179656 | tf_op jit(solution)/shard_map/ppermute | solution.py:19
  62.4 22.8 %collective-permute-start.16 = (bf16[4,3,64,256]{3,2,1,0:T(8,128)(2,1)}, bf16[4,3,64,256]{3,2,1,0:T(8,128)(2,1)}, u32[]{:S(2)}, u32[]{:S(2)}) collective-permute-start(bf16[4,3,64,256]{3,2,1,0:T(8,128)(2,1)} %bitcast.30.refs_8_), channel_id=1, source_target_pairs={{0,8},{8,0},{16,24},{24,16},{1,9},{9,1},{17,25},{25,17},{2,10},{10... | collective-permute-start | bytes 1179656 | tf_op jit(solution)/shard_map/ppermute | solution.py:19
  63.7 32.7 %collective-permute-start.17 = (bf16[4,3,64,256]{3,2,1,0:T(8,128)(2,1)}, bf16[4,3,64,256]{3,2,1,0:T(8,128)(2,1)S(1)}, u32[]{:S(2)}, u32[]{:S(2)}) collective-permute-start(bf16[4,3,64,256]{3,2,1,0:T(8,128)(2,1)} %bitcast.30.refs_8_), channel_id=1, source_target_pairs={{0,16},{8,24},{16,0},{24,8},{1,17},{9,25},{17,1},{25,9},{2,18},{10... | collective-permute-start | bytes 1179656 | tf_op jit(solution)/shard_map/ppermute | solution.py:19
  68.3 30.6 %collective-permute-start.18 = (bf16[4,3,64,256]{3,2,1,0:T(8,128)(2,1)}, bf16[4,3,64,256]{3,2,1,0:T(8,128)(2,1)}, u32[]{:S(2)}, u32[]{:S(2)}) collective-permute-start(bf16[4,3,64,256]{3,2,1,0:T(8,128)(2,1)} %bitcast.30.refs_8_), channel_id=1, source_target_pairs={{0,24},{8,16},{16,8},{24,0},{1,25},{9,17},{17,9},{25,1},{2,26},{10... | collective-permute-start | bytes 1179656 | tf_op jit(solution)/shard_map/ppermute | solution.py:19
  79.6 26.1 %collective-permute-start.23 = (bf16[4,3,64,256]{3,2,1,0:T(8,128)(2,1)S(1)}, bf16[4,3,64,256]{3,2,1,0:T(8,128)(2,1)}, u32[]{:S(2)}, u32[]{:S(2)}) collective-permute-start(bf16[4,3,64,256]{3,2,1,0:T(8,128)(2,1)S(1)} %bitcast.176), channel_id=1, source_target_pairs={{0,8},{8,0},{16,24},{24,16},{1,9},{9,1},{17,25},{25,17},{2,10},{10... | collective-permute-start | bytes 1179656 | tf_op jit(solution)/shard_map/ppermute | solution.py:19
  79.6 30.1 %collective-permute-start.24 = (bf16[4,3,64,256]{3,2,1,0:T(8,128)(2,1)S(1)}, bf16[4,3,64,256]{3,2,1,0:T(8,128)(2,1)}, u32[]{:S(2)}, u32[]{:S(2)}) collective-permute-start(bf16[4,3,64,256]{3,2,1,0:T(8,128)(2,1)S(1)} %bitcast.177), channel_id=1, source_target_pairs={{0,16},{8,24},{16,0},{24,8},{1,17},{9,25},{17,1},{25,9},{2,18},{10... | collective-permute-start | bytes 1179656 | tf_op jit(solution)/shard_map/ppermute | solution.py:19
  85.2 24.5 %collective-permute-start.25 = (bf16[4,3,64,256]{3,2,1,0:T(8,128)(2,1)S(1)}, bf16[4,3,64,256]{3,2,1,0:T(8,128)(2,1)}, u32[]{:S(2)}, u32[]{:S(2)}) collective-permute-start(bf16[4,3,64,256]{3,2,1,0:T(8,128)(2,1)S(1)} %bitcast.178), channel_id=1, source_target_pairs={{0,24},{8,16},{16,8},{24,0},{1,25},{9,17},{17,9},{25,1},{2,26},{10... | collective-permute-start | bytes 1179656 | tf_op jit(solution)/shard_map/ppermute | solution.py:19
  97.2 31.9 %collective-permute-start.12 = (f32[384,256]{1,0:T(8,128)}, f32[384,256]{1,0:T(8,128)S(1)}, u32[]{:S(2)}, u32[]{:S(2)}) collective-permute-start(f32[384,256]{1,0:T(8,128)} %shard_map.60), channel_id=1, source_target_pairs={{0,4},{1,5},{2,6},{3,7},{4,0},{5,1},{6,2},{7,3},{8,12},{9,13},{10,... | collective-permute-start | bytes 1179656 | tf_op jit(solution)/shard_map/ppermute | solution.py:15
  104.1 33.4 %collective-permute-start.19 = (f32[384,256]{1,0:T(8,128)}, f32[384,256]{1,0:T(8,128)S(1)}, u32[]{:S(2)}, u32[]{:S(2)}) collective-permute-start(f32[384,256]{1,0:T(8,128)} %get-tuple-element.7), channel_id=1, source_target_pairs={{0,4},{1,5},{2,6},{3,7},{4,0},{5,1},{6,2},{7,3},{8,12},{9,13},{10,... | collective-permute-start | bytes 1179656 | tf_op jit(solution)/shard_map/ppermute | solution.py:15
  114.8 26.8 %collective-permute-start.26 = (f32[384,256]{1,0:T(8,128)}, f32[384,256]{1,0:T(8,128)S(1)}, u32[]{:S(2)}, u32[]{:S(2)}) collective-permute-start(f32[384,256]{1,0:T(8,128)} %get-tuple-element.9), channel_id=1, source_target_pairs={{0,4},{1,5},{2,6},{3,7},{4,0},{5,1},{6,2},{7,3},{8,12},{9,13},{10,... | collective-permute-start | bytes 1179656 | tf_op jit(solution)/shard_map/ppermute | solution.py:15
  130.5 25.7 %collective-permute-start.28 = (f32[1,128,256]{2,1,0:T(8,128)S(1)}, f32[1,128,256]{2,1,0:T(8,128)S(1)}, u32[]{:S(2)}, u32[]{:S(2)}) collective-permute-start(f32[1,128,256]{2,1,0:T(8,128)S(1)} %get-tuple-element.30), channel_id=1, source_target_pairs={{0,8},{8,0},{16,24},{24,16},{1,9},{9,1},{17,25},{25,17},{2,10},{10... | collective-permute-start | bytes 393224 | tf_op jit(solution)/shard_map/ppermute | solution.py:19
  132.1 25.7 %collective-permute-start.29 = (f32[1,128,256]{2,1,0:T(8,128)S(1)}, f32[1,128,256]{2,1,0:T(8,128)S(1)}, u32[]{:S(2)}, u32[]{:S(2)}) collective-permute-start(f32[1,128,256]{2,1,0:T(8,128)S(1)} %get-tuple-element.32), channel_id=1, source_target_pairs={{0,16},{8,24},{16,0},{24,8},{1,17},{9,25},{17,1},{25,9},{2,18},{10... | collective-permute-start | bytes 393224 | tf_op jit(solution)/shard_map/ppermute | solution.py:19
  150.5 10.9 %collective-permute-start.31 = (f32[1,128,256]{2,1,0:T(8,128)S(1)}, f32[1,128,256]{2,1,0:T(8,128)S(1)}, u32[]{:S(2)}, u32[]{:S(2)}) collective-permute-start(f32[1,128,256]{2,1,0:T(8,128)S(1)} %get-tuple-element.33), channel_id=1, source_target_pairs={{0,8},{8,0},{16,24},{24,16},{1,9},{9,1},{17,25},{25,17},{2,10},{10... | collective-permute-start | bytes 393224 | tf_op jit(solution)/shard_map/ppermute | solution.py:19
  158.0 9.9 %collective-permute-start.41 = (f32[1,32,256]{2,1,0:T(8,128)S(1)}, f32[1,32,256]{2,1,0:T(8,128)S(1)}, u32[]{:S(2)}, u32[]{:S(2)}) collective-permute-start(f32[1,32,256]{2,1,0:T(8,128)S(1)} %get-tuple-element.64), channel_id=1, source_target_pairs={{0,4},{1,5},{2,6},{3,7},{4,0},{5,1},{6,2},{7,3},{8,12},{9,13},{10,... | collective-permute-start | bytes 98312 | tf_op jit(solution)/shard_map/ppermute | solution.py:15
  (40 other events, 355.9 us)
where the time goes:
time: 174 us
  waiting for transfers between devices  81.4 us (47%)
  starting transfers between devices  56 us (32%)
  Pallas kernels  17.9 us (10%)
  other arithmetic  10.5 us (6%)
  local copies, waits for them, and re-layouts  6.16 us (4%)
    ppermute x26, waiting for transfers between devices, by_col(): return lax.ppermute(x, 'pcol', [(q, q ^ k) for q in range(n_col)])  57.9 us
    ppermute x26, starting transfers between devices, by_col(): return lax.ppermute(x, 'pcol', [(q, q ^ k) for q in range(n_col)])  30 us
    ppermute x18, starting transfers between devices, by_row(): return lax.ppermute(x, 'prow', [(p, p ^ k) for p in range(n_row)])  26.1 us
    ppermute x18, waiting for transfers between devices, by_row(): return lax.ppermute(x, 'prow', [(p, p ^ k) for p in range(n_row)])  23.5 us
    pallas_call x4, Pallas kernels, product(): pl.pallas_call(functools.partial(product_kernel, n_row, count), out_shape...  17.9 us
  transfers between devices with their start and end apart: 44, of which 21 were waited for; matrix products, arithmetic and copies ran while one was open for 7% of the time, Pallas kernels for 10%

commit v1 on v0

--- a/solution.py
+++ b/solution.py
@@ -61,6 +61,7 @@
         in_specs=[pl.BlockSpec(memory_space=pltpu.SMEM)] + [vmem] * ((count + 1) * n_row),
         out_specs=[vmem] * count,
         scratch_shapes=[pltpu.VMEM((depth, half), jnp.bfloat16)],
+        compiler_params=pltpu.CompilerParams(vmem_limit_bytes=54 << 20),
         cost_estimate=pl.CostEstimate(
             flops=2 * count * height * depth * half,
             bytes_accessed=2 * depth * (count * height + half) + 4 * count * height * half,
@@ -129,7 +130,7 @@
     row_mask = jnp.sum(tile_mask[:, None, :] * hits[None], axis=2)
     keep = row_mask.astype(jnp.bfloat16)[:, :, None, None]
     keep32 = keep.astype(jnp.float32)
-    masked = panel[:, :, 0] * keep
+    raw = panel[:, :, 0]
     tile_cols = tile_rows // groups
     anc = jnp.transpose(anc_inverse, (0, 2, 1, 3))
     anc = anc.reshape(tile_rows, tile_cols, groups, members, CORES * sub, -1)
@@ -145,14 +146,17 @@
         for x in kept:
             wide += [x, by_col(x, n_col, 1)]
         blocks.append(wide)
-    other = by_col(masked, n_col, 1)
-    both = jnp.concatenate(
-        [jnp.where(core == 0, masked, other), jnp.where(core == 0, other, masked)], axis=2
-    )
-    narrow = lax.dynamic_slice_in_dim(both, core * half, half, axis=3)
-    narrow = narrow.reshape(sets, tile_cols, groups, CORES * sub, half)
+    other = by_col(raw, n_col, 1)
+    both, narrow = [], []
+    for s in range(sets):
+        low = jnp.where(core == 0, raw[s], other[s]) * keep[s]
+        high = jnp.where(core == 0, other[s], raw[s]) * keep[s]
+        x = jnp.concatenate([low, high], axis=1)
+        both.append((low, high))
+        x = lax.dynamic_slice_in_dim(x, core * half, half, axis=2)
+        narrow.append(x.reshape(tile_cols, groups, CORES * sub, half))
     pos = jnp.stack([place, row_pos ^ (col_pos % n_row)]).astype(jnp.int32)
-    outs, values, diags = [], [], []
+    products = []
     for s in range(sets):
         piece = share_panel(narrow[s], group, groups, members, n_col)
         pieces = share_rows(piece, n_row)
@@ -161,7 +165,11 @@
         else:
             parts = product(pos, blocks[-1:], pieces)
             parts = product(pos, blocks[:-1], pieces) + parts
-        total = reduce_groups(parts, groups, members, n_col)
+        products.append(parts)
+    both = lax.optimization_barrier((both, products[-2:][0]))[0]
+    outs, values, diags = [], [], []
+    for s in range(sets):
+        total = reduce_groups(products[s], groups, members, n_col)
         total = total.reshape(tile_rows, CORES, sub, half)
         image = (-total * keep32[s, :, None]).astype(jnp.bfloat16)
         stay, leave = pick(image, core, 1), pick(image, 1 - core, 1)
@@ -172,7 +180,9 @@
             )
         )
         value = jnp.einsum(
-            "axw,axv->wv", both[s], image.reshape(tile_rows, -1, half),
+            "axw,axv->wv",
+            jnp.concatenate(both[s], axis=1),
+            image.reshape(tile_rows, -1, half),
             preferred_element_type=jnp.float32,
         )
         values.append(reduce_rows(value, row_pos, n_row))

time: 174 us -> 179 us (1.029)
  waiting for transfers between devices: 81.4 us -> 89.4 us
    ppermute x18, waiting for transfers between devices: 23.5 us -> 29.9 us  [by_row(): return lax.ppermute(x, 'prow', [(p, p ^ k) for p in range(n_row)])]
  transfers between devices with their start and end apart: 44 -> 44, of which waited for: 21 -> 24; matrix products, arithmetic and copies ran while one was open for 7% -> 7% of each run, Pallas kernels for 10% -> 10%
where the time goes in v1:
time: 179 us
  waiting for transfers between devices  89.4 us (50%)
  starting transfers between devices  55.9 us (31%)
  Pallas kernels  17.9 us (10%)
  other arithmetic  9.25 us (5%)
  local copies, waits for them, and re-layouts  4.53 us (3%)
    ppermute x26, waiting for transfers between devices, by_col(): return lax.ppermute(x, 'pcol', [(q, q ^ k) for q in range(n_col)])  59.5 us
    ppermute x18, waiting for transfers between devices, by_row(): return lax.ppermute(x, 'prow', [(p, p ^ k) for p in range(n_row)])  29.9 us
    ppermute x26, starting transfers between devices, by_col(): return lax.ppermute(x, 'pcol', [(q, q ^ k) for q in range(n_col)])  29.1 us
    ppermute x18, starting transfers between devices, by_row(): return lax.ppermute(x, 'prow', [(p, p ^ k) for p in range(n_row)])  26.8 us
    pallas_call x4, Pallas kernels, product(): pl.pallas_call(functools.partial(product_kernel, n_row, count), out_shape...  17.9 us
  transfers between devices with their start and end apart: 44, of which 24 were waited for; matrix products, arithmetic and copies ran while one was open for 7% of the time, Pallas kernels for 10%

profile of v1, /device:TPU:0, one launch (start us, length us, event | category | flops | bytes accessed | tf_op | source)
XLA Modules:
  0.0 179.2 jit_solution(690358858481201751)
XLA Ops:
  1.2 2.9 %dynamic-slice_bitcast_fusion = (bf16[6,3,64,256]{3,2,1,0:T(8,128)(2,1)}, bf16[6,3,64,256]{3,2,1,0:T(8,128)(2,1)S(1)}, bf16[6,3,64,256]{3,2,1,0:T(8,128)(2,1)}, bf16[6,3,64,256]{3,2,1,0:T(8,128)(2,1)S(1)}) fusion(bf16[6,3,2,2,64,256]{5,4,3,2,1,0:T(8,128)(2,1)} %bitcast.217, s32[]{:T(128)S(6)} %select_n.198, s32[]{:T(128)S(6)} %select_n.192, ...), kind=kLoop, calls=%fused_computation.4 | loop fusion | bytes 4718608 | tf_op jit(solution)/shard_map/jit(dynamic_index_in_dim)/squeeze | solution.py:139
  4.1 2.7 %collective-permute-start.10 = (bf16[6,3,64,256]{3,2,1,0:T(8,128)(2,1)}, bf16[6,3,64,256]{3,2,1,0:T(8,128)(2,1)S(1)}, u32[]{:S(2)}, u32[]{:S(2)}) collective-permute-start(bf16[6,3,64,256]{3,2,1,0:T(8,128)(2,1)} %get-tuple-element.30), channel_id=1, source_target_pairs={{0,2},{1,3},{2,0},{3,1},{4,6},{5,7},{6,4},{7,5},{8,10},{9,11},{10,... | collective-permute-start | bytes 1769480 | tf_op jit(solution)/shard_map/ppermute | solution.py:15
  9.2 3.0 %collective-permute-start.14 = (bf16[3,64,256]{2,1,0:T(8,128)(2,1)S(1)}, bf16[3,64,256]{2,1,0:T(8,128)(2,1)S(1)}, u32[]{:S(2)}, u32[]{:S(2)}) collective-permute-start(bf16[3,64,256]{2,1,0:T(8,128)(2,1)S(1)} %get-tuple-element.69), channel_id=1, source_target_pairs={{0,4},{1,5},{2,6},{3,7},{4,0},{5,1},{6,2},{7,3},{8,12},{9,13},{10,... | collective-permute-start | bytes 294920 | tf_op jit(solution)/shard_map/ppermute | solution.py:15
  12.3 10.9 %collective-permute-done.10.refs_2_.refs_6_ = bf16[6,3,64,256]{3,2,1,0:T(8,128)(2,1)S(1)} collective-permute-done((bf16[6,3,64,256]{3,2,1,0:T(8,128)(2,1)}, bf16[6,3,64,256]{3,2,1,0:T(8,128)(2,1)S(1)}, u32[]{:S(2)}, u32[]{:S(2)}) %collective-permute-start.10) | collective-permute-done | bytes 589856 | tf_op jit(solution)/shard_map/ppermute | solution.py:15
  25.4 12.2 %collective-permute-done.1.refs_2_ = bf16[6,3,64,256]{3,2,1,0:T(8,128)(2,1)S(1)} collective-permute-done((bf16[6,3,64,256]{3,2,1,0:T(8,128)(2,1)}, bf16[6,3,64,256]{3,2,1,0:T(8,128)(2,1)S(1)}, u32[]{:S(2)}, u32[]{:S(2)}) %collective-permute-start.1) | collective-permute-done | bytes 589856 | tf_op jit(solution)/shard_map/ppermute | solution.py:15
  42.7 3.5 %collective-permute-done.21 = bf16[3,64,256]{2,1,0:T(8,128)(2,1)S(1)} collective-permute-done((bf16[3,64,256]{2,1,0:T(8,128)(2,1)S(1)}, bf16[3,64,256]{2,1,0:T(8,128)(2,1)S(1)}, u32[]{:S(2)}, u32[]{:S(2)}) %collective-permute-start.21) | collective-permute-done | bytes 98336 | tf_op jit(solution)/shard_map/ppermute | solution.py:15
  50.5 3.4 %collective-permute-done.5 = bf16[2,3,64,256]{3,2,1,0:T(8,128)(2,1)S(1)} collective-permute-done((bf16[2,3,64,256]{3,2,1,0:T(8,128)(2,1)S(1)}, bf16[2,3,64,256]{3,2,1,0:T(8,128)(2,1)S(1)}, u32[]{:S(2)}, u32[]{:S(2)}) %collective-permute-start.5) | collective-permute-done | bytes 196640 | tf_op jit(solution)/shard_map/ppermute | solution.py:15
  62.9 3.3 %collective-permute-done.16.refs_9_ = bf16[4,3,64,256]{3,2,1,0:T(8,128)(2,1)} collective-permute-done((bf16[4,3,64,256]{3,2,1,0:T(8,128)(2,1)}, bf16[4,3,64,256]{3,2,1,0:T(8,128)(2,1)}, u32[]{:S(2)}, u32[]{:S(2)}) %collective-permute-start.16) | collective-permute-done | bytes 393248 | tf_op jit(solution)/shard_map/ppermute | solution.py:19
  70.7 3.9 %collective-permute-done.6.refs_5_ = bf16[4,3,64,256]{3,2,1,0:T(8,128)(2,1)S(1)} collective-permute-done((bf16[4,3,64,256]{3,2,1,0:T(8,128)(2,1)S(1)}, bf16[4,3,64,256]{3,2,1,0:T(8,128)(2,1)S(1)}, u32[]{:S(2)}, u32[]{:S(2)}) %collective-permute-start.6) | collective-permute-done | bytes 393248 | tf_op jit(solution)/shard_map/ppermute | solution.py:19
  77.8 6.6 %collective-permute-done.8.refs_7_ = bf16[4,3,64,256]{3,2,1,0:T(8,128)(2,1)} collective-permute-done((bf16[4,3,64,256]{3,2,1,0:T(8,128)(2,1)S(1)}, bf16[4,3,64,256]{3,2,1,0:T(8,128)(2,1)}, u32[]{:S(2)}, u32[]{:S(2)}) %collective-permute-start.8) | collective-permute-done | bytes 393248 | tf_op jit(solution)/shard_map/ppermute | solution.py:19
  85.8 3.7 %shard_map.60 = f32[384,256]{1,0:T(8,128)} custom-call(s32[2]{0:T(128)} %pad_add_fusion.pos, bf16[6,3,64,256]{3,2,1,0:T(8,128)(2,1)} %copy-done.1, bf16[6,3,64,256]{3,2,1,0:T(8,128)(2,1)} %copy-done.5, bf16[6,3,64,256]{3,2,1,0:T(8,128)(2,1)} %copy-done.4, bf16[6,3,64,256]{3,2,1,0:T(8,128)(2,1)} %copy-done.7, bf16[4,3,64,256]{3,2,1,0:T(8,128)(2,1)} %bitcast.215, ...), custom_call_target="tpu_custom_call" | custom-call | flops 603979776 | bytes 4325376 | tf_op jit(solution)/shard_map/pallas_call | solution.py:58
  89.5 5.1 %collective-permute-done.17.refs_10_ = bf16[4,3,64,256]{3,2,1,0:T(8,128)(2,1)} collective-permute-done((bf16[4,3,64,256]{3,2,1,0:T(8,128)(2,1)}, bf16[4,3,64,256]{3,2,1,0:T(8,128)(2,1)}, u32[]{:S(2)}, u32[]{:S(2)}) %collective-permute-start.17) | collective-permute-done | bytes 393248 | tf_op jit(solution)/shard_map/ppermute | solution.py:19
  96.8 5.1 %shard_map.61 = (f32[384,256]{1,0:T(8,128)}, f32[384,256]{1,0:T(8,128)}) custom-call(s32[2]{0:T(128)} %pad_add_fusion.pos, bf16[6,3,64,256]{3,2,1,0:T(8,128)(2,1)} %copy-done, bf16[6,3,64,256]{3,2,1,0:T(8,128)(2,1)} %copy-done.3, bf16[6,3,64,256]{3,2,1,0:T(8,128)(2,1)} %copy-done.2, bf16[6,3,64,256]{3,2,1,0:T(8,128)(2,1)} %copy-done.6, ...), custom_call_target="tpu_custom_call" | custom-call | flops 1207959552 | bytes 7077888 | tf_op jit(solution)/shard_map/pallas_call | solution.py:58
  103.2 5.7 %collective-permute-done.24.refs_10_ = bf16[4,3,64,256]{3,2,1,0:T(8,128)(2,1)} collective-permute-done((bf16[4,3,64,256]{3,2,1,0:T(8,128)(2,1)}, bf16[4,3,64,256]{3,2,1,0:T(8,128)(2,1)}, u32[]{:S(2)}, u32[]{:S(2)}) %collective-permute-start.24) | collective-permute-done | bytes 393248 | tf_op jit(solution)/shard_map/ppermute | solution.py:19
  108.9 5.3 %shard_map.62 = (f32[384,256]{1,0:T(8,128)}, f32[384,256]{1,0:T(8,128)}) custom-call(s32[2]{0:T(128)} %pad_add_fusion.pos, bf16[6,3,64,256]{3,2,1,0:T(8,128)(2,1)} %copy-done, bf16[6,3,64,256]{3,2,1,0:T(8,128)(2,1)} %copy-done.3, bf16[6,3,64,256]{3,2,1,0:T(8,128)(2,1)} %copy-done.2, bf16[6,3,64,256]{3,2,1,0:T(8,128)(2,1)} %copy-done.6, ...), custom_call_target="tpu_custom_call" | custom-call | flops 1207959552 | bytes 7077888 | tf_op jit(solution)/shard_map/pallas_call | solution.py:58
  114.2 2.8 %collective-permute-start.26 = (f32[384,256]{1,0:T(8,128)}, f32[384,256]{1,0:T(8,128)S(1)}, u32[]{:S(2)}, u32[]{:S(2)}) collective-permute-start(f32[384,256]{1,0:T(8,128)} %get-tuple-element.15), channel_id=1, source_target_pairs={{0,4},{1,5},{2,6},{3,7},{4,0},{5,1},{6,2},{7,3},{8,12},{9,13},{10,... | collective-permute-start | bytes 1179656 | tf_op jit(solution)/shard_map/ppermute | solution.py:15
  116.9 3.7 %shard_map.59 = f32[384,256]{1,0:T(8,128)} custom-call(s32[2]{0:T(128)} %pad_add_fusion.pos, bf16[6,3,64,256]{3,2,1,0:T(8,128)(2,1)} %copy-done, bf16[6,3,64,256]{3,2,1,0:T(8,128)(2,1)} %copy-done.3, bf16[6,3,64,256]{3,2,1,0:T(8,128)(2,1)} %copy-done.2, bf16[6,3,64,256]{3,2,1,0:T(8,128)(2,1)} %copy-done.6, bf16[4,3,64,256]{3,2,1,0:T(8,128)(2,1)} %bitcast.216, ...), custom_call_target="tpu_custom_call" | custom-call | flops 603979776 | bytes 4325376 | tf_op jit(solution)/shard_map/pallas_call | solution.py:58
  120.7 8.1 %collective-permute-done.12 = f32[384,256]{1,0:T(8,128)S(1)} collective-permute-done((f32[384,256]{1,0:T(8,128)}, f32[384,256]{1,0:T(8,128)S(1)}, u32[]{:S(2)}, u32[]{:S(2)}) %collective-permute-start.12) | collective-permute-done | bytes 393248 | tf_op jit(solution)/shard_map/ppermute | solution.py:15
  133.8 3.4 %collective-permute-done.19 = f32[384,256]{1,0:T(8,128)S(1)} collective-permute-done((f32[384,256]{1,0:T(8,128)}, f32[384,256]{1,0:T(8,128)S(1)}, u32[]{:S(2)}, u32[]{:S(2)}) %collective-permute-start.19) | collective-permute-done | bytes 393248 | tf_op jit(solution)/shard_map/ppermute | solution.py:15
  137.7 6.5 %collective-permute-done.26 = f32[384,256]{1,0:T(8,128)S(1)} collective-permute-done((f32[384,256]{1,0:T(8,128)}, f32[384,256]{1,0:T(8,128)S(1)}, u32[]{:S(2)}, u32[]{:S(2)}) %collective-permute-start.26) | collective-permute-done | bytes 393248 | tf_op jit(solution)/shard_map/ppermute | solution.py:15
  152.7 3.0 %collective-permute-start.30 = (f32[1,128,256]{2,1,0:T(8,128)S(1)}, f32[1,128,256]{2,1,0:T(8,128)S(1)}, u32[]{:S(2)}, u32[]{:S(2)}) collective-permute-start(f32[1,128,256]{2,1,0:T(8,128)S(1)} %get-tuple-element.45), channel_id=1, source_target_pairs={{0,24},{8,16},{16,8},{24,0},{1,25},{9,17},{17,9},{25,1},{2,26},{10... | collective-permute-start | bytes 393224 | tf_op jit(solution)/shard_map/ppermute | solution.py:19
  156.2 3.7 %collective-permute-done.39 = f32[1,128,256]{2,1,0:T(8,128)S(1)} collective-permute-done((f32[1,128,256]{2,1,0:T(8,128)S(1)}, f32[1,128,256]{2,1,0:T(8,128)S(1)}, u32[]{:S(2)}, u32[]{:S(2)}) %collective-permute-start.39) | collective-permute-done | bytes 131104 | tf_op jit(solution)/shard_map/ppermute | solution.py:19
  167.8 3.2 %collective-permute-start.35 = (f32[2,32,256]{2,1,0:T(8,128)S(1)}, f32[2,32,256]{2,1,0:T(8,128)S(1)}, u32[]{:S(2)}, u32[]{:S(2)}) collective-permute-start(f32[2,32,256]{2,1,0:T(8,128)S(1)} %get-tuple-element.61), channel_id=1, source_target_pairs={{0,4},{1,5},{2,6},{3,7},{4,0},{5,1},{6,2},{7,3},{8,12},{9,13},{10,... | collective-permute-start | bytes 196616 | tf_op jit(solution)/shard_map/ppermute | solution.py:15
  172.6 2.8 %collective-permute-done.35 = f32[2,32,256]{2,1,0:T(8,128)S(1)} collective-permute-done((f32[2,32,256]{2,1,0:T(8,128)S(1)}, f32[2,32,256]{2,1,0:T(8,128)S(1)}, u32[]{:S(2)}, u32[]{:S(2)}) %collective-permute-start.35) | collective-permute-done | bytes 65568 | tf_op jit(solution)/shard_map/ppermute | solution.py:15
  (182 shorter events, 63.5 us)
Async XLA Ops:
  4.1 19.2 %collective-permute-start.10 = (bf16[6,3,64,256]{3,2,1,0:T(8,128)(2,1)}, bf16[6,3,64,256]{3,2,1,0:T(8,128)(2,1)S(1)}, u32[]{:S(2)}, u32[]{:S(2)}) collective-permute-start(bf16[6,3,64,256]{3,2,1,0:T(8,128)(2,1)} %get-tuple-element.30), channel_id=1, source_target_pairs={{0,2},{1,3},{2,0},{3,1},{4,6},{5,7},{6,4},{7,5},{8,10},{9,11},{10,... | collective-permute-start | bytes 1769480 | tf_op jit(solution)/shard_map/ppermute | solution.py:15
  6.7 31.0 %collective-permute-start.1 = (bf16[6,3,64,256]{3,2,1,0:T(8,128)(2,1)}, bf16[6,3,64,256]{3,2,1,0:T(8,128)(2,1)S(1)}, u32[]{:S(2)}, u32[]{:S(2)}) collective-permute-start(bf16[6,3,64,256]{3,2,1,0:T(8,128)(2,1)} %get-tuple-element.32), channel_id=1, source_target_pairs={{0,2},{1,3},{2,0},{3,1},{4,6},{5,7},{6,4},{7,5},{8,10},{9,11},{10,... | collective-permute-start | bytes 1769480 | tf_op jit(solution)/shard_map/ppermute | solution.py:15
  6.8 31.4 %collective-permute-start = (bf16[6,3,64,256]{3,2,1,0:T(8,128)(2,1)S(1)}, bf16[6,3,64,256]{3,2,1,0:T(8,128)(2,1)S(1)}, u32[]{:S(2)}, u32[]{:S(2)}) collective-permute-start(bf16[6,3,64,256]{3,2,1,0:T(8,128)(2,1)S(1)} %get-tuple-element.33.refs_0_), channel_id=1, source_target_pairs={{0,1},{1,0},{2,3},{3,2},{4,5},{5,4},{6,7},{7,6},{8,9},{9,8},{10,11... | collective-permute-start | bytes 1769480 | tf_op jit(solution)/shard_map/ppermute | solution.py:15
  6.9 48.8 %collective-permute-start.9 = (bf16[6,3,64,256]{3,2,1,0:T(8,128)(2,1)S(1)}, bf16[6,3,64,256]{3,2,1,0:T(8,128)(2,1)S(1)}, u32[]{:S(2)}, u32[]{:S(2)}) collective-permute-start(bf16[6,3,64,256]{3,2,1,0:T(8,128)(2,1)S(1)} %get-tuple-element.31.refs_0_.refs_4_), channel_id=1, source_target_pairs={{0,1},{1,0},{2,3},{3,2},{4,5},{5,4},{6,7},{7,6},{8,9},{9,8},{10,11... | collective-permute-start | bytes 1769480 | tf_op jit(solution)/shard_map/ppermute | solution.py:15
  9.2 28.5 %collective-permute-start.14 = (bf16[3,64,256]{2,1,0:T(8,128)(2,1)S(1)}, bf16[3,64,256]{2,1,0:T(8,128)(2,1)S(1)}, u32[]{:S(2)}, u32[]{:S(2)}) collective-permute-start(bf16[3,64,256]{2,1,0:T(8,128)(2,1)S(1)} %get-tuple-element.69), channel_id=1, source_target_pairs={{0,4},{1,5},{2,6},{3,7},{4,0},{5,1},{6,2},{7,3},{8,12},{9,13},{10,... | collective-permute-start | bytes 294920 | tf_op jit(solution)/shard_map/ppermute | solution.py:15
  23.2 17.1 %collective-permute-start.4 = (bf16[3,64,256]{2,1,0:T(8,128)(2,1)S(1)}, bf16[3,64,256]{2,1,0:T(8,128)(2,1)S(1)}, u32[]{:S(2)}, u32[]{:S(2)}) collective-permute-start(bf16[3,64,256]{2,1,0:T(8,128)(2,1)S(1)} %get-tuple-element.65), channel_id=1, source_target_pairs={{0,4},{1,5},{2,6},{3,7},{4,0},{5,1},{6,2},{7,3},{8,12},{9,13},{10,... | collective-permute-start | bytes 294920 | tf_op jit(solution)/shard_map/ppermute | solution.py:15
  37.7 20.9 %collective-permute-start.11 = (bf16[6,3,64,256]{3,2,1,0:T(8,128)(2,1)S(1)}, bf16[6,3,64,256]{3,2,1,0:T(8,128)(2,1)S(1)}, u32[]{:S(2)}, u32[]{:S(2)}) collective-permute-start(bf16[6,3,64,256]{3,2,1,0:T(8,128)(2,1)S(1)} %collective-permute-done.10.refs_2_.refs_6_), channel_id=1, source_target_pairs={{0,1},{1,0},{2,3},{3,2},{4,5},{5,4},{6,7},{7,6},{8,9},{9,8},{10,11... | collective-permute-start | bytes 1769480 | tf_op jit(solution)/shard_map/ppermute | solution.py:15
  37.7 22.4 %collective-permute-start.2 = (bf16[6,3,64,256]{3,2,1,0:T(8,128)(2,1)S(1)}, bf16[6,3,64,256]{3,2,1,0:T(8,128)(2,1)S(1)}, u32[]{:S(2)}, u32[]{:S(2)}) collective-permute-start(bf16[6,3,64,256]{3,2,1,0:T(8,128)(2,1)S(1)} %collective-permute-done.1.refs_2_), channel_id=1, source_target_pairs={{0,1},{1,0},{2,3},{3,2},{4,5},{5,4},{6,7},{7,6},{8,9},{9,8},{10,11... | collective-permute-start | bytes 1769480 | tf_op jit(solution)/shard_map/ppermute | solution.py:15
  54.0 12.3 %collective-permute-start.16 = (bf16[4,3,64,256]{3,2,1,0:T(8,128)(2,1)}, bf16[4,3,64,256]{3,2,1,0:T(8,128)(2,1)}, u32[]{:S(2)}, u32[]{:S(2)}) collective-permute-start(bf16[4,3,64,256]{3,2,1,0:T(8,128)(2,1)} %bitcast.38.refs_8_), channel_id=1, source_target_pairs={{0,8},{8,0},{16,24},{24,16},{1,9},{9,1},{17,25},{25,17},{2,10},{10... | collective-permute-start | bytes 1179656 | tf_op jit(solution)/shard_map/ppermute | solution.py:19
  55.7 18.9 %collective-permute-start.6 = (bf16[4,3,64,256]{3,2,1,0:T(8,128)(2,1)S(1)}, bf16[4,3,64,256]{3,2,1,0:T(8,128)(2,1)S(1)}, u32[]{:S(2)}, u32[]{:S(2)}) collective-permute-start(bf16[4,3,64,256]{3,2,1,0:T(8,128)(2,1)S(1)} %bitcast.212), channel_id=1, source_target_pairs={{0,8},{8,0},{16,24},{24,16},{1,9},{9,1},{17,25},{25,17},{2,10},{10... | collective-permute-start | bytes 1179656 | tf_op jit(solution)/shard_map/ppermute | solution.py:19
  56.9 19.3 %collective-permute-start.7 = (bf16[4,3,64,256]{3,2,1,0:T(8,128)(2,1)S(1)}, bf16[4,3,64,256]{3,2,1,0:T(8,128)(2,1)S(1)}, u32[]{:S(2)}, u32[]{:S(2)}) collective-permute-start(bf16[4,3,64,256]{3,2,1,0:T(8,128)(2,1)S(1)} %bitcast.213), channel_id=1, source_target_pairs={{0,16},{8,24},{16,0},{24,8},{1,17},{9,25},{17,1},{25,9},{2,18},{10... | collective-permute-start | bytes 1179656 | tf_op jit(solution)/shard_map/ppermute | solution.py:19
  58.6 25.7 %collective-permute-start.8 = (bf16[4,3,64,256]{3,2,1,0:T(8,128)(2,1)S(1)}, bf16[4,3,64,256]{3,2,1,0:T(8,128)(2,1)}, u32[]{:S(2)}, u32[]{:S(2)}) collective-permute-start(bf16[4,3,64,256]{3,2,1,0:T(8,128)(2,1)S(1)} %bitcast.214), channel_id=1, source_target_pairs={{0,24},{8,16},{16,8},{24,0},{1,25},{9,17},{17,9},{25,1},{2,26},{10... | collective-permute-start | bytes 1179656 | tf_op jit(solution)/shard_map/ppermute | solution.py:19
  60.9 33.8 %collective-permute-start.17 = (bf16[4,3,64,256]{3,2,1,0:T(8,128)(2,1)}, bf16[4,3,64,256]{3,2,1,0:T(8,128)(2,1)}, u32[]{:S(2)}, u32[]{:S(2)}) collective-permute-start(bf16[4,3,64,256]{3,2,1,0:T(8,128)(2,1)} %bitcast.38.refs_8_), channel_id=1, source_target_pairs={{0,16},{8,24},{16,0},{24,8},{1,17},{9,25},{17,1},{25,9},{2,18},{10... | collective-permute-start | bytes 1179656 | tf_op jit(solution)/shard_map/ppermute | solution.py:19
  66.3 30.5 %collective-permute-start.18 = (bf16[4,3,64,256]{3,2,1,0:T(8,128)(2,1)}, bf16[4,3,64,256]{3,2,1,0:T(8,128)(2,1)}, u32[]{:S(2)}, u32[]{:S(2)}) collective-permute-start(bf16[4,3,64,256]{3,2,1,0:T(8,128)(2,1)} %bitcast.38.refs_8_), channel_id=1, source_target_pairs={{0,24},{8,16},{16,8},{24,0},{1,25},{9,17},{17,9},{25,1},{2,26},{10... | collective-permute-start | bytes 1179656 | tf_op jit(solution)/shard_map/ppermute | solution.py:19
  74.6 28.6 %collective-permute-start.23 = (bf16[4,3,64,256]{3,2,1,0:T(8,128)(2,1)}, bf16[4,3,64,256]{3,2,1,0:T(8,128)(2,1)}, u32[]{:S(2)}, u32[]{:S(2)}) collective-permute-start(bf16[4,3,64,256]{3,2,1,0:T(8,128)(2,1)} %bitcast.55.refs_8_), channel_id=1, source_target_pairs={{0,8},{8,0},{16,24},{24,16},{1,9},{9,1},{17,25},{25,17},{2,10},{10... | collective-permute-start | bytes 1179656 | tf_op jit(solution)/shard_map/ppermute | solution.py:19
  76.3 32.7 %collective-permute-start.24 = (bf16[4,3,64,256]{3,2,1,0:T(8,128)(2,1)}, bf16[4,3,64,256]{3,2,1,0:T(8,128)(2,1)}, u32[]{:S(2)}, u32[]{:S(2)}) collective-permute-start(bf16[4,3,64,256]{3,2,1,0:T(8,128)(2,1)} %bitcast.55.refs_8_), channel_id=1, source_target_pairs={{0,16},{8,24},{16,0},{24,8},{1,17},{9,25},{17,1},{25,9},{2,18},{10... | collective-permute-start | bytes 1179656 | tf_op jit(solution)/shard_map/ppermute | solution.py:19
  84.3 24.6 %collective-permute-start.25 = (bf16[4,3,64,256]{3,2,1,0:T(8,128)(2,1)}, bf16[4,3,64,256]{3,2,1,0:T(8,128)(2,1)}, u32[]{:S(2)}, u32[]{:S(2)}) collective-permute-start(bf16[4,3,64,256]{3,2,1,0:T(8,128)(2,1)} %bitcast.55.refs_8_), channel_id=1, source_target_pairs={{0,24},{8,16},{16,8},{24,0},{1,25},{9,17},{17,9},{25,1},{2,26},{10... | collective-permute-start | bytes 1179656 | tf_op jit(solution)/shard_map/ppermute | solution.py:19
  94.7 34.1 %collective-permute-start.12 = (f32[384,256]{1,0:T(8,128)}, f32[384,256]{1,0:T(8,128)S(1)}, u32[]{:S(2)}, u32[]{:S(2)}) collective-permute-start(f32[384,256]{1,0:T(8,128)} %shard_map.60), channel_id=1, source_target_pairs={{0,4},{1,5},{2,6},{3,7},{4,0},{5,1},{6,2},{7,3},{8,12},{9,13},{10,... | collective-permute-start | bytes 1179656 | tf_op jit(solution)/shard_map/ppermute | solution.py:15
  101.9 35.2 %collective-permute-start.19 = (f32[384,256]{1,0:T(8,128)}, f32[384,256]{1,0:T(8,128)S(1)}, u32[]{:S(2)}, u32[]{:S(2)}) collective-permute-start(f32[384,256]{1,0:T(8,128)} %get-tuple-element.13), channel_id=1, source_target_pairs={{0,4},{1,5},{2,6},{3,7},{4,0},{5,1},{6,2},{7,3},{8,12},{9,13},{10,... | collective-permute-start | bytes 1179656 | tf_op jit(solution)/shard_map/ppermute | solution.py:15
  114.2 30.0 %collective-permute-start.26 = (f32[384,256]{1,0:T(8,128)}, f32[384,256]{1,0:T(8,128)S(1)}, u32[]{:S(2)}, u32[]{:S(2)}) collective-permute-start(f32[384,256]{1,0:T(8,128)} %get-tuple-element.15), channel_id=1, source_target_pairs={{0,4},{1,5},{2,6},{3,7},{4,0},{5,1},{6,2},{7,3},{8,12},{9,13},{10,... | collective-permute-start | bytes 1179656 | tf_op jit(solution)/shard_map/ppermute | solution.py:15
  130.3 29.7 %collective-permute-start.28 = (f32[1,128,256]{2,1,0:T(8,128)S(1)}, f32[1,128,256]{2,1,0:T(8,128)S(1)}, u32[]{:S(2)}, u32[]{:S(2)}) collective-permute-start(f32[1,128,256]{2,1,0:T(8,128)S(1)} %get-tuple-element.44), channel_id=1, source_target_pairs={{0,8},{8,0},{16,24},{24,16},{1,9},{9,1},{17,25},{25,17},{2,10},{10... | collective-permute-start | bytes 393224 | tf_op jit(solution)/shard_map/ppermute | solution.py:19
  131.9 30.2 %collective-permute-start.29 = (f32[1,128,256]{2,1,0:T(8,128)S(1)}, f32[1,128,256]{2,1,0:T(8,128)S(1)}, u32[]{:S(2)}, u32[]{:S(2)}) collective-permute-start(f32[1,128,256]{2,1,0:T(8,128)S(1)} %get-tuple-element.46), channel_id=1, source_target_pairs={{0,16},{8,24},{16,0},{24,8},{1,17},{9,25},{17,1},{25,9},{2,18},{10... | collective-permute-start | bytes 393224 | tf_op jit(solution)/shard_map/ppermute | solution.py:19
  152.7 10.0 %collective-permute-start.30 = (f32[1,128,256]{2,1,0:T(8,128)S(1)}, f32[1,128,256]{2,1,0:T(8,128)S(1)}, u32[]{:S(2)}, u32[]{:S(2)}) collective-permute-start(f32[1,128,256]{2,1,0:T(8,128)S(1)} %get-tuple-element.45), channel_id=1, source_target_pairs={{0,24},{8,16},{16,8},{24,0},{1,25},{9,17},{17,9},{25,1},{2,26},{10... | collective-permute-start | bytes 393224 | tf_op jit(solution)/shard_map/ppermute | solution.py:19
  155.7 9.6 %collective-permute-start.31 = (f32[1,128,256]{2,1,0:T(8,128)S(1)}, f32[1,128,256]{2,1,0:T(8,128)S(1)}, u32[]{:S(2)}, u32[]{:S(2)}) collective-permute-start(f32[1,128,256]{2,1,0:T(8,128)S(1)} %get-tuple-element.47), channel_id=1, source_target_pairs={{0,8},{8,0},{16,24},{24,16},{1,9},{9,1},{17,25},{25,17},{2,10},{10... | collective-permute-start | bytes 393224 | tf_op jit(solution)/shard_map/ppermute | solution.py:19
  (47 other events, 770.2 us)
